TPU v7x, 512 devices: a whole 4x8x8 slice. The times are simulated.
512 devices in a mesh: dp: 2 (over core), ctx: 64 (over z, y), head: 4 (over x).
Axes of the slice: x: 4, y: 8, z: 8, core: 2. Of those that a mesh axis runs over, the one named last changes fastest.
Arguments:
- queries: bfloat16 [2, 8192, 2560], P('dp', 'ctx', 'head'), may hold values from -25 to 25
- keys: bfloat16 [2, 8192, 2560], P('dp', 'ctx', 'head'), may hold values from -25 to 25
- values: bfloat16 [2, 8192, 2560], P('dp', 'ctx', 'head'), may hold values from -6 to 6
- grad_y: bfloat16 [2, 8192, 2560], P('dp', 'ctx', 'head'), may hold values from -6 to 6
- out_gain: float32 [2560], P('head'), may hold values from 0.1 to 1.9
- offsets: int32 [2, 20], P(None, 'head'), may hold values from 0 to 63, as said below
Outputs:
- attended: bfloat16 [2, 8192, 2560], P('dp', 'ctx', 'head')
- query_grad: bfloat16 [2, 8192, 2560], P('dp', 'ctx', 'head')
- key_grad: bfloat16 [2, 8192, 2560], P('dp', 'ctx', 'head')
- value_grad: bfloat16 [2, 8192, 2560], P('dp', 'ctx', 'head')
- gain_grad: float32 [2560], P('head')
Inputs may be any that keep to these rules, and one draw needn't show every extreme that they name: Row 0 holds offsets below 8, row 1 offsets below 64.
All inputs are finite; a program needn't handle non-finite values.
Results may differ from a plain program's by a relative error of at most 0.011.
Values may be sent and summed in bfloat16 or wider, within the bound.
A program may use at most 64 MiB of HBM per device.

v0:
```python
import math
import jax
import jax.numpy as jnp
from jax import lax
from jax.sharding import PartitionSpec as P

HEAD_DIM = 128
SPAN = 4
R1 = 8
EPS = 1e-06


def group_gather(block, axis, group):
    count = lax.axis_size(axis)
    pieces = [block]
    for shift in range(1, group):
        route = []
        for src in range(count):
            base = src - src % group
            route.append((src, base + (src % group + shift) % group))
        pieces.append(lax.ppermute(block, axis, route))
    return jnp.concatenate(pieces, 0)


def pick_rows(source_rows, dilation, shifts):
    row_count, head_count, head_width = source_rows.shape
    grouped = source_rows.reshape(row_count // dilation, dilation, head_count, head_width)
    hit_mask = jnp.arange(dilation, dtype=jnp.int32).reshape(1, dilation, 1, 1) == shifts.reshape(
        1, 1, head_count, 1
    )
    chosen = jnp.where(hit_mask, grouped, jnp.zeros((), source_rows.dtype))
    return jnp.sum(chosen, axis=1, dtype=source_rows.dtype)


def place_rows(row_values, dilation, shifts):
    row_count, head_count, head_width = row_values.shape
    hit_mask = jnp.arange(dilation, dtype=jnp.int32).reshape(1, dilation, 1, 1) == shifts.reshape(
        1, 1, head_count, 1
    )
    spread = jnp.where(hit_mask, row_values[:, None], jnp.zeros((), row_values.dtype))
    return spread.reshape(row_count * dilation, head_count, head_width)


def level_scores(q_rows, k_rows):
    score_scale = 1.0 / math.sqrt(q_rows.shape[-1])
    return (
        jnp.einsum("qhe,khe->hqk", q_rows, k_rows, preferred_element_type=jnp.float32) * score_scale
    )


def attend(q_rows, k_rows, v_rows):
    scores = level_scores(q_rows, k_rows)
    row_max = jnp.max(scores, axis=-1, keepdims=True)
    log_total = row_max[..., 0] + jnp.log(jnp.sum(jnp.exp(scores - row_max), axis=-1))
    soft_rows = jnp.exp(scores - log_total[..., None]).astype(jnp.bfloat16)
    level_out = jnp.einsum("hqk,khe->qhe", soft_rows, v_rows, preferred_element_type=jnp.float32)
    return (level_out, log_total.T)


def score_grads(q_rows, k_rows, v_rows, log_total, grad_low, row_shift):
    score_scale = 1.0 / math.sqrt(q_rows.shape[-1])
    scores = level_scores(q_rows, k_rows)
    exact_soft = jnp.exp(scores - log_total.T[..., None])
    prob_grad = jnp.einsum("qhe,khe->hqk", grad_low, v_rows, preferred_element_type=jnp.float32)
    score_grad = (exact_soft * (prob_grad + row_shift.T[..., None]) * score_scale).astype(
        jnp.bfloat16
    )
    return (score_grad, exact_soft.astype(jnp.bfloat16))


def key_parts(score_grad, soft_low, q_rows, grad_low):
    k_part = jnp.einsum("hqk,qhe->khe", score_grad, q_rows, preferred_element_type=jnp.float32)
    v_part = jnp.einsum("hqk,qhe->khe", soft_low, grad_low, preferred_element_type=jnp.float32)
    return (k_part, v_part)


def query_part(score_grad, k_rows):
    return jnp.einsum("hqk,khe->qhe", score_grad, k_rows, preferred_element_type=jnp.float32)


def split_qkv(packed, head_count):
    width = head_count * HEAD_DIM
    shape = (packed.shape[0], head_count, HEAD_DIM)
    return tuple((packed[:, i * width : (i + 1) * width].reshape(shape) for i in range(3)))


def pack_grads(grad_low, row_shift):
    rows = grad_low.shape[0]
    return jnp.concatenate(
        [grad_low.astype(jnp.float32).reshape(rows, -1), row_shift.astype(jnp.float32)], 1
    )


def unpack_grads(packed, head_count):
    width = head_count * HEAD_DIM
    grad_low = packed[:, :width].astype(jnp.bfloat16).reshape(-1, head_count, HEAD_DIM)
    return (grad_low, packed[:, width:])


def shards(queries, keys, values, grad_y, out_gain, offsets):
    tokens = queries.shape[1]
    flat_width = queries.shape[2]
    head_count = flat_width // HEAD_DIM
    row_shape = (tokens, head_count, HEAD_DIM)
    q_own = queries[0].reshape(row_shape)
    k_own = keys[0].reshape(row_shape)
    v_own = values[0].reshape(row_shape)
    ctx_size = lax.axis_size("ctx")
    my_place = lax.axis_index("ctx")
    mid_shift = offsets[0]
    top_shift = offsets[1]
    positions = jnp.arange(tokens, dtype=jnp.int32)
    mid_hit = (positions % R1)[:, None] == mid_shift[None, :]
    top_hit = (positions % ctx_size)[:, None] == top_shift[None, :]
    mid_pack = jnp.concatenate(
        [pick_rows(x, R1, mid_shift).reshape(-1, flat_width) for x in (q_own, k_own, v_own)], 1
    )
    top_pack = jnp.concatenate(
        [pick_rows(x, ctx_size, top_shift).reshape(-1, flat_width) for x in (q_own, k_own, v_own)],
        1,
    )
    mid_rows = mid_pack.shape[0]
    top_rows = top_pack.shape[0]
    mid_all = group_gather(mid_pack, "ctx", SPAN)
    top_all = lax.all_gather(top_pack, "ctx", axis=0, tiled=True)
    mid_q, mid_k, mid_v = split_qkv(mid_all, head_count)
    top_q, top_k, top_v = split_qkv(top_all, head_count)
    top_start = my_place * top_rows
    base_out, base_total = attend(q_own, k_own, v_own)
    mid_out_all, mid_total_all = attend(mid_q, mid_k, mid_v)
    top_out_all, top_total_all = attend(top_q, top_k, top_v)
    mid_out = mid_out_all[:mid_rows]
    mid_total = mid_total_all[:mid_rows]
    top_out = lax.dynamic_slice_in_dim(top_out_all, top_start, top_rows, 0)
    top_total = lax.dynamic_slice_in_dim(top_total_all, top_start, top_rows, 0)
    mid_full = place_rows(mid_total[..., None], R1, mid_shift)[..., 0]
    top_full = place_rows(top_total[..., None], ctx_size, top_shift)[..., 0]
    row_max = jnp.maximum(base_total, jnp.where(mid_hit, mid_full, base_total))
    row_max = jnp.maximum(row_max, jnp.where(top_hit, top_full, base_total))
    base_expo = jnp.exp(base_total - row_max)
    mid_expo = jnp.where(mid_hit, jnp.exp(mid_full - row_max), 0.0)
    top_expo = jnp.where(top_hit, jnp.exp(top_full - row_max), 0.0)
    denom = base_expo + mid_expo + top_expo
    base_share = base_expo / denom
    mid_share = mid_expo / denom
    top_share = top_expo / denom
    attn = (
        base_share[..., None] * base_out
        + mid_share[..., None] * place_rows(mid_out, R1, mid_shift)
        + top_share[..., None] * place_rows(top_out, ctx_size, top_shift)
    )
    inv_rms = lax.rsqrt(jnp.mean(attn * attn, axis=-1, keepdims=True) + EPS)
    normed = attn * inv_rms
    gain_rows = out_gain.reshape(head_count, HEAD_DIM)
    attended = (normed * gain_rows).astype(jnp.bfloat16).reshape(1, tokens, flat_width)
    grad_full = grad_y[0].reshape(row_shape).astype(jnp.float32)
    gain_part = jnp.sum(grad_full * normed, axis=0).reshape(flat_width)
    gain_grad = lax.psum(gain_part, ("dp", "ctx"))
    grad_norm = grad_full * gain_rows
    grad_attn = inv_rms * (
        grad_norm - normed * jnp.mean(grad_norm * normed, axis=-1, keepdims=True)
    )
    inner = jnp.sum(grad_attn * attn, axis=-1)
    base_low = (base_share[..., None] * grad_attn).astype(jnp.bfloat16)
    base_shift = -(base_share * inner)
    base_grad, base_soft = score_grads(q_own, k_own, v_own, base_total, base_low, base_shift)
    base_dq = query_part(base_grad, k_own)
    base_dk, base_dv = key_parts(base_grad, base_soft, q_own, base_low)
    mid_sel = pick_rows(mid_share[..., None], R1, mid_shift)[..., 0]
    mid_low = (mid_sel[..., None] * pick_rows(grad_attn, R1, mid_shift)).astype(jnp.bfloat16)
    mid_row_shift = -(mid_sel * pick_rows(inner[..., None], R1, mid_shift)[..., 0])
    top_sel = pick_rows(top_share[..., None], ctx_size, top_shift)[..., 0]
    top_low = (top_sel[..., None] * pick_rows(grad_attn, ctx_size, top_shift)).astype(jnp.bfloat16)
    top_row_shift = -(top_sel * pick_rows(inner[..., None], ctx_size, top_shift)[..., 0])
    mid_low_all, mid_shift_all = unpack_grads(
        group_gather(pack_grads(mid_low, mid_row_shift), "ctx", SPAN), head_count
    )
    top_low_all, top_shift_all = unpack_grads(
        lax.all_gather(pack_grads(top_low, top_row_shift), "ctx", axis=0, tiled=True), head_count
    )
    mid_grad, mid_soft = score_grads(mid_q, mid_k, mid_v, mid_total_all, mid_low_all, mid_shift_all)
    mid_dq = query_part(mid_grad[:, :mid_rows], mid_k)
    mid_dk, mid_dv = key_parts(
        mid_grad[:, :, :mid_rows], mid_soft[:, :, :mid_rows], mid_q, mid_low_all
    )
    top_grad, top_soft = score_grads(top_q, top_k, top_v, top_total_all, top_low_all, top_shift_all)
    own_grad = lax.dynamic_slice_in_dim(top_grad, top_start, top_rows, 1)
    top_dq = query_part(own_grad, top_k)
    key_grad_cols = lax.dynamic_slice_in_dim(top_grad, top_start, top_rows, 2)
    key_soft_cols = lax.dynamic_slice_in_dim(top_soft, top_start, top_rows, 2)
    top_dk, top_dv = key_parts(key_grad_cols, key_soft_cols, top_q, top_low_all)
    query_grad = (
        base_dq + place_rows(mid_dq, R1, mid_shift) + place_rows(top_dq, ctx_size, top_shift)
    )
    key_grad = base_dk + place_rows(mid_dk, R1, mid_shift) + place_rows(top_dk, ctx_size, top_shift)
    value_grad = (
        base_dv + place_rows(mid_dv, R1, mid_shift) + place_rows(top_dv, ctx_size, top_shift)
    )
    out_shape = (1, tokens, flat_width)
    return (
        attended,
        query_grad.astype(jnp.bfloat16).reshape(out_shape),
        key_grad.astype(jnp.bfloat16).reshape(out_shape),
        value_grad.astype(jnp.bfloat16).reshape(out_shape),
        gain_grad,
    )


def solution(mesh):
    in_specs = (
        P("dp", "ctx", "head"),
        P("dp", "ctx", "head"),
        P("dp", "ctx", "head"),
        P("dp", "ctx", "head"),
        P("head"),
        P(None, "head"),
    )
    out_specs = (
        P("dp", "ctx", "head"),
        P("dp", "ctx", "head"),
        P("dp", "ctx", "head"),
        P("dp", "ctx", "head"),
        P("head"),
    )
    return jax.shard_map(shards, mesh=mesh, in_specs=in_specs, out_specs=out_specs, check_vma=False)
```

profile of v0, /device:TPU:256, one launch (start us, length us, event | category | flops | bytes accessed | tf_op | source)
XLA Modules:
  0.0 428.5 jit_solution(14037007713612233846)
XLA Ops:
  0.6 0.8 slice_bitcast_fusion.5
  1.4 0.6 copy-done.23
  2.0 1.5 fusion.24
  3.6 5.5 %collective-permute-start.2 = (bf16[16,1920]{1,0:T(8,128)(2,1)S(1)}, bf16[16,1920]{1,0:T(8,128)(2,1)S(1)}, u32[]{:S(2)}, u32[]{:S(2)}) collective-permute-start(bf16[16,1920]{1,0:T(8,128)(2,1)S(1)} %bitcast_dynamic-update-slice_fusion), channel_id=1, source_target_pairs={{0,12},{4,0},{8,4},{12,8},{16,28},{20,16},{24,20},{28,24},{32,44},... | collective-permute-start | bytes 184328 | tf_op jit(solution)/shard_map/ppermute | solution.py:21
  9.1 1.9 collective-permute-start.1
  11.0 2.9 collective-permute-start
  14.1 0.7 copy-done.1
  15.1 0.7 copy-done.2
  17.2 0.7 broadcast_in_dim.285
  17.9 0.6 broadcast_in_dim.278
  19.2 50.0 %all-gather = bf16[64,2,1920]{2,1,0:T(2,128)(2,1)S(1)} all-gather(bf16[1,2,1920]{2,1,0:T(2,128)(2,1)S(1)} %maximum_bitcast_fusion.1), channel_id=1, replica_groups=mesh['dp'=2,'ctx'=64,'head'=4] {'ctx'}, dimensions={0}, use_global_device_ids=true | all-gather | bytes 499200 | tf_op jit(solution)/shard_map/all_gather | solution.py:125
  71.0 0.7 broadcast_in_dim.289
  72.8 0.5 copy-done.9
  75.5 0.7 copy-done.13
  76.1 0.8 multiply_reduce_fusion
  76.9 0.7 copy-done.15
  78.0 0.6 negate_bitcast_fusion
  79.1 0.6 pad_maximum_fusion.2
  79.7 2.6 collective-permute-start.5
  82.3 3.1 collective-permute-start.4
  85.4 2.3 collective-permute-start.3
  88.7 49.2 %all-gather.1 = f32[64,2,645]{2,1,0:T(2,128)S(1)} all-gather(f32[1,2,645]{2,1,0:T(2,128)S(1)} %maximum_bitcast_fusion.2), channel_id=1, replica_groups=mesh['dp'=2,'ctx'=64,'head'=4] {'ctx'}, dimensions={0}, use_global_device_ids=true | all-gather | bytes 335400 | tf_op jit(solution)/shard_map/all_gather | solution.py:179
  138.2 0.7 slice.99
  141.7 0.8 copy.357
  143.2 277.9 %psum.7 = f32[640]{0:T(1024)} all-reduce(f32[640]{0:T(1024)S(1)} %bitcast.273), channel_id=1, replica_groups=mesh['dp'=2,'ctx'=64,'head'=4] {'dp','ctx'}, use_global_device_ids=true, to_apply=%region_22.23 | all-reduce | flops 640 | bytes 5120 | tf_op jit(solution)/shard_map/psum | solution.py:158
  421.1 0.9 pad_maximum_fusion.1
  422.1 0.8 maximum_bitcast_fusion
  423.0 0.5 copy-done.10
  424.1 0.6 copy-done.12
  425.1 0.8 copy.359
  426.4 0.8 copy.358
  427.7 0.8 copy.360
  (144 shorter events, 15.0 us)
Async XLA Ops:
  1.4 0.6 copy-start.23
  1.4 15.2 %copy-start.25 = (s32[5]{0:T(128)}, s32[5]{0:T(128)S(1)}, u32[]{:S(2)}) copy-start(s32[5]{0:T(128)S(1)} %get-tuple-element.62) | copy-start | bytes 64
  2.0 15.9 %copy-start.14 = (pred[8,5]{0,1:T(8,128)(4,1)}, pred[8,5]{0,1:T(8,128)(4,1)S(1)}, u32[]{:S(2)}) copy-start(pred[8,5]{0,1:T(8,128)(4,1)S(1)} %iota_compare_fusion.1) | copy-start | bytes 124
  2.0 11.9 %copy-start = (bf16[1,128,640]{2,1,0:T(8,128)(2,1)S(1)}, bf16[1,128,640]{2,1,0:T(8,128)(2,1)}, u32[]{:S(2)}) copy-start(bf16[1,128,640]{2,1,0:T(8,128)(2,1)} %param.6) | copy-start | bytes 491524
  3.6 68.8 %collective-permute-start.2 = (bf16[16,1920]{1,0:T(8,128)(2,1)S(1)}, bf16[16,1920]{1,0:T(8,128)(2,1)S(1)}, u32[]{:S(2)}, u32[]{:S(2)}) collective-permute-start(bf16[16,1920]{1,0:T(8,128)(2,1)S(1)} %bitcast_dynamic-update-slice_fusion), channel_id=1, source_target_pairs={{0,12},{4,0},{8,4},{12,8},{16,28},{20,16},{24,20},{28,24},{32,44},... | collective-permute-start | bytes 184328 | tf_op jit(solution)/shard_map/ppermute | solution.py:21
  9.1 63.3 %collective-permute-start.1 = (bf16[16,1920]{1,0:T(8,128)(2,1)S(1)}, bf16[16,1920]{1,0:T(8,128)(2,1)S(1)}, u32[]{:S(2)}, u32[]{:S(2)}) collective-permute-start(bf16[16,1920]{1,0:T(8,128)(2,1)S(1)} %bitcast_dynamic-update-slice_fusion), channel_id=1, source_target_pairs={{0,8},{4,12},{8,0},{12,4},{16,24},{20,28},{24,16},{28,20},{32,40},... | collective-permute-start | bytes 184328 | tf_op jit(solution)/shard_map/ppermute | solution.py:21
  11.0 61.3 %collective-permute-start = (bf16[16,1920]{1,0:T(8,128)(2,1)S(1)}, bf16[16,1920]{1,0:T(8,128)(2,1)S(1)}, u32[]{:S(2)}, u32[]{:S(2)}) collective-permute-start(bf16[16,1920]{1,0:T(8,128)(2,1)S(1)} %bitcast_dynamic-update-slice_fusion), channel_id=1, source_target_pairs={{0,4},{4,8},{8,12},{12,0},{16,20},{20,24},{24,28},{28,16},{32,36},... | collective-permute-start | bytes 184328 | tf_op jit(solution)/shard_map/ppermute | solution.py:21
  14.0 0.9 copy-start.1
  14.9 0.9 copy-start.2
  16.4 2.2 copy-start.6
  70.3 0.6 copy-start.7
  72.4 1.0 copy-start.4
  72.7 0.6 copy-start.9
  73.5 0.7 copy-start.19
  73.5 0.7 copy-start.26
  73.7 0.7 copy-start.18
  73.7 0.7 copy-start.11
  73.8 0.7 copy-start.24
  75.4 0.7 copy-start.13
  76.9 0.7 copy-start.15
  79.7 341.3 %collective-permute-start.5 = (f32[16,645]{1,0:T(8,128)}, f32[16,645]{1,0:T(8,128)}, u32[]{:S(2)}, u32[]{:S(2)}) collective-permute-start(f32[16,645]{1,0:T(8,128)} %pad_maximum_fusion.2), channel_id=1, source_target_pairs={{0,12},{4,0},{8,4},{12,8},{16,28},{20,16},{24,20},{28,24},{32,44},... | collective-permute-start | bytes 123848 | tf_op jit(solution)/shard_map/ppermute | solution.py:21
  82.3 338.8 %collective-permute-start.4 = (f32[16,645]{1,0:T(8,128)}, f32[16,645]{1,0:T(8,128)}, u32[]{:S(2)}, u32[]{:S(2)}) collective-permute-start(f32[16,645]{1,0:T(8,128)} %pad_maximum_fusion.2), channel_id=1, source_target_pairs={{0,8},{4,12},{8,0},{12,4},{16,24},{20,28},{24,16},{28,20},{32,40},... | collective-permute-start | bytes 123848 | tf_op jit(solution)/shard_map/ppermute | solution.py:21
  85.4 335.7 %collective-permute-start.3 = (f32[16,645]{1,0:T(8,128)}, f32[16,645]{1,0:T(8,128)}, u32[]{:S(2)}, u32[]{:S(2)}) collective-permute-start(f32[16,645]{1,0:T(8,128)} %pad_maximum_fusion.2), channel_id=1, source_target_pairs={{0,4},{4,8},{8,12},{12,0},{16,20},{20,24},{24,28},{28,16},{32,36},... | collective-permute-start | bytes 123848 | tf_op jit(solution)/shard_map/ppermute | solution.py:21
  87.7 0.6 copy-start.22
  138.2 0.7 copy-start.16
  138.9 0.9 copy-start.3
  140.0 0.7 copy-start.8
  141.7 0.8 copy-start.20
  142.5 0.7 copy-start.17
  422.1 0.9 copy-start.5
  422.8 0.7 copy-start.10
  424.1 0.6 copy-start.12
  (1 other events, 0.5 us)
where the time goes:
time: 429 us
  blocking collectives  377 us (88%)
  local copies, waits for them, and re-layouts  19.9 us (5%)
  starting transfers between devices  18.3 us (4%)
  other arithmetic  7.42 us (2%)
  matrix products  4.56 us (1%)
    psum x1, blocking collectives, shards(): gain_grad = lax.psum(gain_part, ('dp', 'ctx'))  278 us
    all_gather x1, blocking collectives, shards(): top_all = lax.all_gather(top_pack, 'ctx', axis=0, tiled=True)  50 us
    all_gather x1, blocking collectives, shards(): lax.all_gather(pack_grads(top_low, top_row_shift), 'ctx', axis=0, tiled=T...  49.2 us
    ppermute x6, starting transfers between devices, group_gather(): pieces.append(lax.ppermute(block, axis, route))  18.3 us
    unnamed x69, local copies, waits for them, and re-layouts  13.1 us
  transfers between devices with their start and end apart: 6, of which 0 were waited for; matrix products, arithmetic and copies ran while one was open for 2% of the time, Pallas kernels for 0%

commit v1 on v0

--- a/solution.py
+++ b/solution.py
@@ -8,6 +8,11 @@
 SPAN = 4
 R1 = 8
 EPS = 1e-06
+
+
+def axis_by_axis(array, first, second):
+    partial = lax.psum(array, first)
+    return lax.psum(partial, second)
 
 
 def group_gather(block, axis, group):
@@ -155,7 +160,7 @@
     attended = (normed * gain_rows).astype(jnp.bfloat16).reshape(1, tokens, flat_width)
     grad_full = grad_y[0].reshape(row_shape).astype(jnp.float32)
     gain_part = jnp.sum(grad_full * normed, axis=0).reshape(flat_width)
-    gain_grad = lax.psum(gain_part, ("dp", "ctx"))
+    gain_grad = axis_by_axis(gain_part, "ctx", "dp")
     grad_norm = grad_full * gain_rows
     grad_attn = inv_rms * (
         grad_norm - normed * jnp.mean(grad_norm * normed, axis=-1, keepdims=True)

time: 429 us -> 304 us (0.71)
  the two profiles are of different devices: /device:TPU:256 before, /device:TPU:1 now
where the time goes in v1:
time: 304 us; the launch traced here: 303 us
  blocking collectives  251 us (83%)
  local copies, waits for them, and re-layouts  19.9 us (7%)
  starting transfers between devices  19 us (6%)
  other arithmetic  7.42 us (2%)
  matrix products  4.56 us (1%)
    psum x1, blocking collectives, axis_by_axis(): partial = lax.psum(array, first)  113 us
    psum x1, blocking collectives, axis_by_axis(): return lax.psum(partial, second)  55.9 us
    all_gather x1, blocking collectives, shards(): top_all = lax.all_gather(top_pack, 'ctx', axis=0, tiled=True)  44.2 us
    all_gather x1, blocking collectives, shards(): lax.all_gather(pack_grads(top_low, top_row_shift), 'ctx', axis=0, tiled=T...  37.9 us
    ppermute x6, starting transfers between devices, group_gather(): pieces.append(lax.ppermute(block, axis, route))  19 us
    unnamed x69, local copies, waits for them, and re-layouts  13.1 us
  transfers between devices with their start and end apart: 6, of which 0 were waited for; matrix products, arithmetic and copies ran while one was open for 3% of the time, Pallas kernels for 0%

profile of v1, /device:TPU:1, one launch (start us, length us, event | category | flops | bytes accessed | tf_op | source)
XLA Modules:
  0.0 303.0 jit_solution(10014502177558052411)
XLA Ops:
  0.6 0.8 slice_bitcast_fusion.5
  1.4 0.6 copy-done.23
  2.0 1.5 fusion.24
  3.6 6.1 %collective-permute-start.2 = (bf16[16,1920]{1,0:T(8,128)(2,1)S(1)}, bf16[16,1920]{1,0:T(8,128)(2,1)S(1)}, u32[]{:S(2)}, u32[]{:S(2)}) collective-permute-start(bf16[16,1920]{1,0:T(8,128)(2,1)S(1)} %bitcast_dynamic-update-slice_fusion), channel_id=1, source_target_pairs={{0,12},{4,0},{8,4},{12,8},{16,28},{20,16},{24,20},{28,24},{32,44},... | collective-permute-start | bytes 184328 | tf_op jit(solution)/shard_map/ppermute | solution.py:26
  9.7 1.9 collective-permute-start.1
  11.6 2.3 collective-permute-start
  14.1 0.7 copy-done.1
  15.0 0.7 copy-done.2
  17.2 0.7 broadcast_in_dim.285
  17.9 0.6 broadcast_in_dim.278
  19.2 44.2 %all-gather = bf16[64,2,1920]{2,1,0:T(2,128)(2,1)S(1)} all-gather(bf16[1,2,1920]{2,1,0:T(2,128)(2,1)S(1)} %maximum_bitcast_fusion.1), channel_id=1, replica_groups=mesh['dp'=2,'ctx'=64,'head'=4] {'ctx'}, dimensions={0}, use_global_device_ids=true | all-gather | bytes 499200 | tf_op jit(solution)/shard_map/all_gather | solution.py:130
  65.2 0.7 broadcast_in_dim.289
  66.9 0.5 copy-done.9
  69.6 0.7 copy-done.13
  70.3 0.8 multiply_reduce_fusion
  71.1 0.7 copy-done.15
  72.2 0.6 negate_bitcast_fusion
  73.2 0.6 pad_maximum_fusion.2
  73.9 3.9 %collective-permute-start.5 = (f32[16,645]{1,0:T(8,128)}, f32[16,645]{1,0:T(8,128)}, u32[]{:S(2)}, u32[]{:S(2)}) collective-permute-start(f32[16,645]{1,0:T(8,128)} %pad_maximum_fusion.2), channel_id=1, source_target_pairs={{0,12},{4,0},{8,4},{12,8},{16,28},{20,16},{24,20},{28,24},{32,44},... | collective-permute-start | bytes 123848 | tf_op jit(solution)/shard_map/ppermute | solution.py:26
  77.8 2.8 collective-permute-start.4
  80.6 1.9 collective-permute-start.3
  83.5 37.9 %all-gather.1 = f32[64,2,645]{2,1,0:T(2,128)S(1)} all-gather(f32[1,2,645]{2,1,0:T(2,128)S(1)} %maximum_bitcast_fusion.2), channel_id=1, replica_groups=mesh['dp'=2,'ctx'=64,'head'=4] {'ctx'}, dimensions={0}, use_global_device_ids=true | all-gather | bytes 335400 | tf_op jit(solution)/shard_map/all_gather | solution.py:184
  121.7 0.7 slice.99
  125.2 0.8 copy.357
  126.7 113.0 %psum.14 = f32[640]{0:T(1024)S(1)} all-reduce(f32[640]{0:T(1024)S(1)} %bitcast.273), channel_id=1, replica_groups=mesh['dp'=2,'ctx'=64,'head'=4] {'ctx'}, use_global_device_ids=true, to_apply=%region_22.23 | all-reduce | flops 640 | bytes 5120 | tf_op jit(solution)/shard_map/psum | solution.py:14
  239.7 55.9 %psum.15 = f32[640]{0:T(1024)} all-reduce(f32[640]{0:T(1024)S(1)} %psum.14), channel_id=1, replica_groups=mesh['dp'=2,'ctx'=64,'head'=4] {'dp'}, use_global_device_ids=true, to_apply=%region_23.24 | all-reduce | flops 640 | bytes 5120 | tf_op jit(solution)/shard_map/psum | solution.py:15
  295.6 0.9 pad_maximum_fusion.1
  296.6 0.8 maximum_bitcast_fusion
  298.6 0.6 copy-done.12
  299.7 0.8 copy.359
  300.9 0.8 copy.358
  302.2 0.8 copy.360
  (145 shorter events, 15.5 us)
Async XLA Ops:
  1.4 0.6 copy-start.23
  1.4 15.2 %copy-start.25 = (s32[5]{0:T(128)}, s32[5]{0:T(128)S(1)}, u32[]{:S(2)}) copy-start(s32[5]{0:T(128)S(1)} %get-tuple-element.62) | copy-start | bytes 64
  2.0 15.9 %copy-start.14 = (pred[8,5]{0,1:T(8,128)(4,1)}, pred[8,5]{0,1:T(8,128)(4,1)S(1)}, u32[]{:S(2)}) copy-start(pred[8,5]{0,1:T(8,128)(4,1)S(1)} %iota_compare_fusion.1) | copy-start | bytes 124
  2.0 11.9 %copy-start = (bf16[1,128,640]{2,1,0:T(8,128)(2,1)S(1)}, bf16[1,128,640]{2,1,0:T(8,128)(2,1)}, u32[]{:S(2)}) copy-start(bf16[1,128,640]{2,1,0:T(8,128)(2,1)} %param.6) | copy-start | bytes 491524
  3.6 62.9 %collective-permute-start.2 = (bf16[16,1920]{1,0:T(8,128)(2,1)S(1)}, bf16[16,1920]{1,0:T(8,128)(2,1)S(1)}, u32[]{:S(2)}, u32[]{:S(2)}) collective-permute-start(bf16[16,1920]{1,0:T(8,128)(2,1)S(1)} %bitcast_dynamic-update-slice_fusion), channel_id=1, source_target_pairs={{0,12},{4,0},{8,4},{12,8},{16,28},{20,16},{24,20},{28,24},{32,44},... | collective-permute-start | bytes 184328 | tf_op jit(solution)/shard_map/ppermute | solution.py:26
  9.7 56.9 %collective-permute-start.1 = (bf16[16,1920]{1,0:T(8,128)(2,1)S(1)}, bf16[16,1920]{1,0:T(8,128)(2,1)S(1)}, u32[]{:S(2)}, u32[]{:S(2)}) collective-permute-start(bf16[16,1920]{1,0:T(8,128)(2,1)S(1)} %bitcast_dynamic-update-slice_fusion), channel_id=1, source_target_pairs={{0,8},{4,12},{8,0},{12,4},{16,24},{20,28},{24,16},{28,20},{32,40},... | collective-permute-start | bytes 184328 | tf_op jit(solution)/shard_map/ppermute | solution.py:26
  11.6 55.0 %collective-permute-start = (bf16[16,1920]{1,0:T(8,128)(2,1)S(1)}, bf16[16,1920]{1,0:T(8,128)(2,1)S(1)}, u32[]{:S(2)}, u32[]{:S(2)}) collective-permute-start(bf16[16,1920]{1,0:T(8,128)(2,1)S(1)} %bitcast_dynamic-update-slice_fusion), channel_id=1, source_target_pairs={{0,4},{4,8},{8,12},{12,0},{16,20},{20,24},{24,28},{28,16},{32,36},... | collective-permute-start | bytes 184328 | tf_op jit(solution)/shard_map/ppermute | solution.py:26
  14.0 0.9 copy-start.1
  14.9 0.9 copy-start.2
  16.4 2.2 copy-start.6
  64.5 0.6 copy-start.7
  66.6 1.0 copy-start.4
  66.9 0.6 copy-start.9
  67.6 0.7 copy-start.19
  67.7 0.7 copy-start.26
  67.9 0.7 copy-start.18
  67.9 0.7 copy-start.11
  67.9 0.7 copy-start.24
  69.6 0.7 copy-start.13
  71.1 0.7 copy-start.15
  73.9 221.7 %collective-permute-start.5 = (f32[16,645]{1,0:T(8,128)}, f32[16,645]{1,0:T(8,128)}, u32[]{:S(2)}, u32[]{:S(2)}) collective-permute-start(f32[16,645]{1,0:T(8,128)} %pad_maximum_fusion.2), channel_id=1, source_target_pairs={{0,12},{4,0},{8,4},{12,8},{16,28},{20,16},{24,20},{28,24},{32,44},... | collective-permute-start | bytes 123848 | tf_op jit(solution)/shard_map/ppermute | solution.py:26
  77.8 217.8 %collective-permute-start.4 = (f32[16,645]{1,0:T(8,128)}, f32[16,645]{1,0:T(8,128)}, u32[]{:S(2)}, u32[]{:S(2)}) collective-permute-start(f32[16,645]{1,0:T(8,128)} %pad_maximum_fusion.2), channel_id=1, source_target_pairs={{0,8},{4,12},{8,0},{12,4},{16,24},{20,28},{24,16},{28,20},{32,40},... | collective-permute-start | bytes 123848 | tf_op jit(solution)/shard_map/ppermute | solution.py:26
  80.6 215.0 %collective-permute-start.3 = (f32[16,645]{1,0:T(8,128)}, f32[16,645]{1,0:T(8,128)}, u32[]{:S(2)}, u32[]{:S(2)}) collective-permute-start(f32[16,645]{1,0:T(8,128)} %pad_maximum_fusion.2), channel_id=1, source_target_pairs={{0,4},{4,8},{8,12},{12,0},{16,20},{20,24},{24,28},{28,16},{32,36},... | collective-permute-start | bytes 123848 | tf_op jit(solution)/shard_map/ppermute | solution.py:26
  82.5 0.6 copy-start.22
  121.7 0.7 copy-start.16
  122.4 0.9 copy-start.3
  123.5 0.7 copy-start.8
  125.2 0.8 copy-start.20
  126.0 0.7 copy-start.17
  296.6 0.9 copy-start.5
  297.4 0.7 copy-start.10
  298.6 0.6 copy-start.12
  (1 other events, 0.5 us)
